TPU v7x, 512 devices: a whole 4x4x16 slice. The times are simulated.
512 devices in a mesh: src: 32 (over y, x, core), tgt: 16 (over z).
Axes of the slice: x: 4, y: 4, z: 16, core: 2. Of those that a mesh axis runs over, the one named last changes fastest.
Arguments:
- src_cells: float32 [50, 131072], P(None, ('src', 'tgt')), may hold values from -0.8 to 0.8
- tgt_cells: float32 [50, 8192], P(None, 'tgt'), may hold values from -0.8 to 0.8
- src_mass: float32 [131072], P('src'), may hold values from 0.5 to 2
- tgt_mass: float32 [8192], P('tgt'), may hold values from 0.5 to 2
Outputs:
- src_potential: float32 [131072], P('src')
- tgt_potential: float32 [8192], P('tgt')
All inputs are finite; a program needn't handle non-finite values.
Results may differ from a plain program's by a relative error of at most 0.00015.
Values sent between devices are 32-bit elements; how exact they have to be, the bound alone decides.
No kernel may reach another device: no remote copies, remote signals or barrier semaphores. Data moves between devices by JAX's collectives and lax.ppermute only.
A program may use at most 64 MiB of HBM per device.

v0:
```python
import jax
import jax.numpy as jnp
from jax import lax
from jax.sharding import PartitionSpec as P

ITERS = 2
epsilon_reg = 2.0


def gibbs_tile(src_block, tgt_block):
    src_norm = jnp.sum(src_block * src_block, axis=0)
    tgt_norm = jnp.sum(tgt_block * tgt_block, axis=0)
    cross = jnp.dot(
        src_block.T, tgt_block, precision=lax.Precision.HIGHEST, preferred_element_type=jnp.float32
    )
    cost = src_norm[:, None] + tgt_norm[None, :] - 2.0 * cross
    return jnp.exp(-cost / epsilon_reg)


def local(src_cells, tgt_cells, src_mass, tgt_mass):
    src_block = lax.all_gather(src_cells, "tgt", axis=1, tiled=True)
    stored_tile = gibbs_tile(src_block, tgt_cells)

    def get_tile():
        return stored_tile

    col_scale = jnp.ones((tgt_cells.shape[1],), jnp.float32)
    row_scale = jnp.ones((src_block.shape[1],), jnp.float32)
    for sweep in range(ITERS):
        row_part = jnp.dot(get_tile(), col_scale, precision=lax.Precision.HIGHEST)
        row_total = lax.psum(row_part, "tgt")
        row_scale = src_mass / row_total
        col_part = jnp.dot(row_scale, get_tile(), precision=lax.Precision.HIGHEST)
        col_total = lax.psum(col_part, "src")
        col_scale = tgt_mass / col_total
    return (epsilon_reg * jnp.log(row_scale), epsilon_reg * jnp.log(col_scale))


def solution(mesh):
    placed = (P(None, ("src", "tgt")), P(None, "tgt"), P("src"), P("tgt"))
    return jax.shard_map(
        local, mesh=mesh, in_specs=placed, out_specs=(P("src"), P("tgt")), check_vma=False
    )
```

profile of v0, /device:TPU:1, one launch (start us, length us, event | category | flops | bytes accessed | tf_op | source)
XLA Modules:
  0.0 317.8 jit_solution(1861517863350990255)
XLA Ops:
  0.6 0.9 multiply_reduce_fusion.1
  1.6 34.9 %all_gather.3 = f32[50,4096]{1,0:T(8,128)S(1)} all-gather(f32[50,256]{1,0:T(8,128)} %param.4), channel_id=1, replica_groups=mesh['src'=32,'tgt'=16] {'tgt'}, dimensions={1}, use_global_device_ids=true | all-gather | bytes 870400 | tf_op jit(solution)/shard_map/all_gather | solution.py:21
  36.4 0.1 multiply_reduce_fusion
  36.5 9.2 %multiply_exponential_fusion = f32[4096,512]{1,0:T(8,128)S(1)} fusion(f32[50,4096]{1,0:T(8,128)S(1)} %all_gather.3, f32[50,512]{1,0:T(8,128)} %param.5, f32[512]{0:T(512)S(1)} %multiply_reduce_fusion.1, f32[4096]{0:T(1024)S(1)} %multiply_reduce_fusion), kind=kOutput, calls=%fused_computation | convolution fusion | flops 1268776960 | bytes 9328640 | tf_op jit(solution)/shard_map/dot_general | solution.py:13
  45.7 0.0 copy-start
  45.7 3.2 %copy-done = f32[4096,512]{1,0:T(8,128)} copy-done((f32[4096,512]{1,0:T(8,128)}, f32[4096,512]{1,0:T(8,128)S(1)}, u32[]{:S(2)}) %copy-start) | copy-done | bytes 8388632
  48.9 0.0 copy-start.1
  48.9 0.0 copy-start.2
  48.9 7.3 %fusion = f32[1,4096]{1,0:T(1,128)S(1)} fusion(f32[4096,512]{1,0:T(8,128)S(1)} %multiply_exponential_fusion), kind=kOutput, calls=%fused_computation.5 | convolution fusion | flops 25165824 | bytes 8404992 | tf_op jit(solution)/shard_map/dot_general | solution.py:30
  56.2 38.9 %psum.28 = f32[4096]{0:T(1024)S(1)} all-reduce(f32[4096]{0:T(1024)S(1)} %bitcast.18), channel_id=1, replica_groups=mesh['src'=32,'tgt'=16] {'tgt'}, use_global_device_ids=true, to_apply=%region_2.0 | all-reduce | flops 4096 | bytes 32768 | tf_op jit(solution)/shard_map/psum | solution.py:31
  95.1 0.0 copy-done.1
  95.1 6.4 %fusion.3 = f32[1,512]{1,0:T(1,128)S(1)} fusion(f32[4096,1]{0,1:T(1,128)S(1)} %bitcast.16, f32[4096,512]{1,0:T(8,128)} %copy-done), kind=kOutput, calls=%fused_computation.8 | convolution fusion | flops 25165824 | bytes 8407040 | tf_op jit(solution)/shard_map/dot_general | solution.py:33
  101.5 83.6 %psum.29 = f32[512]{0:T(512)S(1)} all-reduce(f32[512]{0:T(512)S(1)} %bitcast.22), channel_id=1, replica_groups=mesh['src'=32,'tgt'=16] {'src'}, use_global_device_ids=true, to_apply=%region_3.0 | all-reduce | flops 512 | bytes 4096 | tf_op jit(solution)/shard_map/psum | solution.py:34
  185.1 0.0 copy-done.2
  185.1 9.4 %fusion.4 = f32[1,4096]{1,0:T(1,128)S(1)} fusion(f32[4096,512]{1,0:T(8,128)} %copy-done, f32[512,1]{0,1:T(1,128)S(1)} %bitcast.20), kind=kOutput, calls=%fused_computation.9 | convolution fusion | flops 25165824 | bytes 8407040 | tf_op jit(solution)/shard_map/dot_general | solution.py:30
  194.6 39.5 %psum.30 = f32[4096]{0:T(1024)S(1)} all-reduce(f32[4096]{0:T(1024)S(1)} %bitcast.17), channel_id=1, replica_groups=mesh['src'=32,'tgt'=16] {'tgt'}, use_global_device_ids=true, to_apply=%region_4.0 | all-reduce | flops 4096 | bytes 32768 | tf_op jit(solution)/shard_map/psum | solution.py:31
  234.1 0.6 log_multiply_fusion
  234.7 6.4 %fusion.5 = f32[1,512]{1,0:T(1,128)S(1)} fusion(f32[4096,1]{0,1:T(1,128)S(1)} %bitcast.19, f32[4096,512]{1,0:T(8,128)} %copy-done), kind=kOutput, calls=%fused_computation.10 | convolution fusion | flops 25165824 | bytes 8407040 | tf_op jit(solution)/shard_map/dot_general | solution.py:33
  241.1 76.1 %psum.31 = f32[512]{0:T(512)S(1)} all-reduce(f32[512]{0:T(512)S(1)} %bitcast.21), channel_id=1, replica_groups=mesh['src'=32,'tgt'=16] {'src'}, use_global_device_ids=true, to_apply=%region_5.0 | all-reduce | flops 512 | bytes 4096 | tf_op jit(solution)/shard_map/psum | solution.py:34
  317.2 0.6 log_multiply_fusion.1
  (2 shorter events, 0.0 us)
Async XLA Ops:
  45.7 3.2 %copy-start = (f32[4096,512]{1,0:T(8,128)}, f32[4096,512]{1,0:T(8,128)S(1)}, u32[]{:S(2)}) copy-start(f32[4096,512]{1,0:T(8,128)S(1)} %multiply_exponential_fusion) | copy-start | bytes 25165828
  48.9 46.2 %copy-start.1 = (f32[4096]{0:T(1024)S(1)}, f32[4096]{0:T(1024)}, u32[]{:S(2)}) copy-start(f32[4096]{0:T(1024)} %param.6) | copy-start | bytes 49156
  48.9 136.2 %copy-start.2 = (f32[512]{0:T(512)S(1)}, f32[512]{0:T(512)}, u32[]{:S(2)}) copy-start(f32[512]{0:T(512)} %param.7) | copy-start | bytes 6148
where the time goes:
time: 318 us
  blocking collectives  273 us (86%)
  matrix products  38.6 us (12%)
  local copies, waits for them, and re-layouts  3.22 us (1%)
    psum x2, blocking collectives, local(): col_total = lax.psum(col_part, 'src')  160 us
    psum x2, blocking collectives, local(): row_total = lax.psum(row_part, 'tgt')  78.5 us
    all_gather x1, blocking collectives, local(): src_block = lax.all_gather(src_cells, 'tgt', axis=1, tiled=True)  34.9 us
    dot_general x2, matrix products, local(): row_part = jnp.dot(get_tile(), col_scale, precision=lax.Precision.HIGHEST)  16.7 us
    dot_general x2, matrix products, local(): col_part = jnp.dot(row_scale, get_tile(), precision=lax.Precision.HIGHEST)  12.7 us
    dot_general x1, matrix products, gibbs_tile(): jnp.dot(src_block.T, tgt_block, precision=lax.Precision.HIGHEST, preferre...  9.15 us

commit v1 on v0

--- a/solution.py
+++ b/solution.py
@@ -31,7 +31,7 @@
         row_total = lax.psum(row_part, "tgt")
         row_scale = src_mass / row_total
         col_part = jnp.dot(row_scale, get_tile(), precision=lax.Precision.HIGHEST)
-        col_total = lax.psum(col_part, "src")
+        col_total = jnp.sum(lax.all_gather(col_part, "src"), axis=0)
         col_scale = tgt_mass / col_total
     return (epsilon_reg * jnp.log(row_scale), epsilon_reg * jnp.log(col_scale))
 

time: 318 us -> 241 us (0.76)
  blocking collectives: 273 us -> 196 us
    psum x2 -> x0, blocking collectives: 160 us -> none  [local(): col_total = lax.psum(col_part, 'src')]
    all_gather x0 -> x2, blocking collectives: none -> 83 us  [local(): col_total = jnp.sum(lax.all_gather(col_part, 'src'), axis=0)]
where the time goes in v1:
time: 241 us
  blocking collectives  196 us (81%)
  matrix products  38.6 us (16%)
  local copies, waits for them, and re-layouts  3.22 us (1%)
    all_gather x2, blocking collectives, local(): col_total = jnp.sum(lax.all_gather(col_part, 'src'), axis=0)  83 us
    psum x2, blocking collectives, local(): row_total = lax.psum(row_part, 'tgt')  78.2 us
    all_gather x1, blocking collectives, local(): src_block = lax.all_gather(src_cells, 'tgt', axis=1, tiled=True)  34.9 us
    dot_general x2, matrix products, local(): row_part = jnp.dot(get_tile(), col_scale, precision=lax.Precision.HIGHEST)  16.7 us
    dot_general x2, matrix products, local(): col_part = jnp.dot(row_scale, get_tile(), precision=lax.Precision.HIGHEST)  12.7 us
    dot_general x1, matrix products, gibbs_tile(): jnp.dot(src_block.T, tgt_block, precision=lax.Precision.HIGHEST, preferre...  9.15 us

profile of v1, /device:TPU:1, one launch (start us, length us, event | category | flops | bytes accessed | tf_op | source)
XLA Modules:
  0.0 241.0 jit_solution(8193878473444967759)
XLA Ops:
  0.6 0.9 multiply_reduce_fusion.1
  1.6 34.9 %all_gather.15 = f32[50,4096]{1,0:T(8,128)S(1)} all-gather(f32[50,256]{1,0:T(8,128)} %param.4), channel_id=1, replica_groups=mesh['src'=32,'tgt'=16] {'tgt'}, dimensions={1}, use_global_device_ids=true | all-gather | bytes 870400 | tf_op jit(solution)/shard_map/all_gather | solution.py:21
  36.4 0.1 multiply_reduce_fusion
  36.5 9.2 %multiply_exponential_fusion = f32[4096,512]{1,0:T(8,128)S(1)} fusion(f32[50,4096]{1,0:T(8,128)S(1)} %all_gather.15, f32[50,512]{1,0:T(8,128)} %param.5, f32[512]{0:T(512)S(1)} %multiply_reduce_fusion.1, f32[4096]{0:T(1024)S(1)} %multiply_reduce_fusion), kind=kOutput, calls=%fused_computation | convolution fusion | flops 1268776960 | bytes 9328640 | tf_op jit(solution)/shard_map/dot_general | solution.py:13
  45.7 0.0 copy-start
  45.7 3.2 %copy-done = f32[4096,512]{1,0:T(8,128)} copy-done((f32[4096,512]{1,0:T(8,128)}, f32[4096,512]{1,0:T(8,128)S(1)}, u32[]{:S(2)}) %copy-start) | copy-done | bytes 8388632
  48.9 0.0 copy-start.1
  48.9 0.0 copy-start.2
  48.9 7.3 %fusion = f32[1,4096]{1,0:T(1,128)S(1)} fusion(f32[4096,512]{1,0:T(8,128)S(1)} %multiply_exponential_fusion), kind=kOutput, calls=%fused_computation.7 | convolution fusion | flops 25165824 | bytes 8404992 | tf_op jit(solution)/shard_map/dot_general | solution.py:30
  56.2 38.9 %psum.14 = f32[4096]{0:T(1024)S(1)} all-reduce(f32[4096]{0:T(1024)S(1)} %bitcast.24), channel_id=1, replica_groups=mesh['src'=32,'tgt'=16] {'tgt'}, use_global_device_ids=true, to_apply=%region_2.0 | all-reduce | flops 4096 | bytes 32768 | tf_op jit(solution)/shard_map/psum | solution.py:31
  95.1 0.0 copy-done.1
  95.1 6.4 %convolution_bitcast_fusion.1 = f32[1,1,512]{2,1,0:T(1,128)S(1)} fusion(f32[4096,1]{0,1:T(1,128)S(1)} %bitcast.22, f32[4096,512]{1,0:T(8,128)} %copy-done), kind=kOutput, calls=%fused_computation.2 | convolution fusion | flops 25165824 | bytes 8407040 | tf_op jit(solution)/shard_map/dot_general | solution.py:33
  101.5 45.6 %all-gather.2 = f32[32,1,512]{2,1,0:T(1,128)S(1)} all-gather(f32[1,1,512]{2,1,0:T(1,128)S(1)} %convolution_bitcast_fusion.1), channel_id=2, replica_groups=mesh['src'=32,'tgt'=16] {'src'}, dimensions={0}, use_global_device_ids=true | all-gather | bytes 67584 | tf_op jit(solution)/shard_map/all_gather | solution.py:34
  147.1 0.1 reduce_sum.38
  147.2 0.0 copy-done.2
  147.2 9.4 %fusion.3 = f32[1,4096]{1,0:T(1,128)S(1)} fusion(f32[4096,512]{1,0:T(8,128)} %copy-done, f32[512,1]{0,1:T(1,128)S(1)} %bitcast.26), kind=kOutput, calls=%fused_computation.10 | convolution fusion | flops 25165824 | bytes 8407040 | tf_op jit(solution)/shard_map/dot_general | solution.py:30
  156.6 39.3 %psum.15 = f32[4096]{0:T(1024)S(1)} all-reduce(f32[4096]{0:T(1024)S(1)} %bitcast.23), channel_id=1, replica_groups=mesh['src'=32,'tgt'=16] {'tgt'}, use_global_device_ids=true, to_apply=%region_4.0 | all-reduce | flops 4096 | bytes 32768 | tf_op jit(solution)/shard_map/psum | solution.py:31
  196.0 0.6 log_multiply_fusion
  196.6 6.4 %convolution_bitcast_fusion = f32[1,1,512]{2,1,0:T(1,128)S(1)} fusion(f32[4096,1]{0,1:T(1,128)S(1)} %bitcast.25, f32[4096,512]{1,0:T(8,128)} %copy-done), kind=kOutput, calls=%fused_computation.1 | convolution fusion | flops 25165824 | bytes 8407040 | tf_op jit(solution)/shard_map/dot_general | solution.py:33
  202.9 37.4 %all-gather.3 = f32[32,1,512]{2,1,0:T(1,128)S(1)} all-gather(f32[1,1,512]{2,1,0:T(1,128)S(1)} %convolution_bitcast_fusion), channel_id=3, replica_groups=mesh['src'=32,'tgt'=16] {'src'}, dimensions={0}, use_global_device_ids=true | all-gather | bytes 67584 | tf_op jit(solution)/shard_map/all_gather | solution.py:34
  240.3 0.1 reduce_sum.39
  240.4 0.6 log_multiply_fusion.1
  (2 shorter events, 0.0 us)
Async XLA Ops:
  45.7 3.2 %copy-start = (f32[4096,512]{1,0:T(8,128)}, f32[4096,512]{1,0:T(8,128)S(1)}, u32[]{:S(2)}) copy-start(f32[4096,512]{1,0:T(8,128)S(1)} %multiply_exponential_fusion) | copy-start | bytes 25165828
  48.9 46.2 %copy-start.1 = (f32[4096]{0:T(1024)S(1)}, f32[4096]{0:T(1024)}, u32[]{:S(2)}) copy-start(f32[4096]{0:T(1024)} %param.6) | copy-start | bytes 49156
  48.9 98.3 %copy-start.2 = (f32[512]{0:T(512)S(1)}, f32[512]{0:T(512)}, u32[]{:S(2)}) copy-start(f32[512]{0:T(512)} %param.7) | copy-start | bytes 6148
